TPU v7x, 1024 devices: a whole 8x8x8 slice. The times are simulated.
1024 devices in a mesh: grp: 16 (over x, z_lo), dom: 64 (over y, z_hi, core).
Axes of the slice: x: 8, y: 8, z: 8 (z_hi: 4, z_lo: 2; z = z_hi * 2 + z_lo), core: 2. Of those that a mesh axis runs over, the one named last changes fastest.
Arguments:
- pert_fcst: bfloat16 [32, 8, 2, 64, 4096], P('grp', None, None, 'dom'), may hold values from -6 to 6
- control: float32 [32, 8, 256, 1024], P('grp', None, 'dom'), may hold values from -6 to 6
- departures: float32 [8, 2, 256, 1024], P(None, None, 'dom'), may hold values from -6 to 6
- obs_weight: float32 [8, 2, 256, 1024], P(None, None, 'dom'), may hold values from 0.3 to 3
- diff_rate: float32 [8], replicated, may hold values from 0.05 to 0.24
- step_counts: int32 [8], replicated, may hold values from 1 to 4, as said below
Outputs:
- increment: float32 [8, 2, 256, 1024], P(None, None, 'dom')
- gradient: float32 [32, 8, 256, 1024], P('grp', None, 'dom')
Inputs may be any that keep to these rules, and one draw needn't show every extreme that they name: `step_counts`: some level has exactly 4 sweeps.
All inputs are finite; a program needn't handle non-finite values.
Results may differ from a plain program's by a relative error of at most 0.0003.
Values may be sent and summed in bfloat16 or wider, within the bound.
A program may use at most 32 MiB of HBM per device.

v0:
```python
import math

import jax
import jax.numpy as jnp
from jax import lax
from jax.sharding import PartitionSpec as P

NSTEP = 4


def extended(block, sides, width):
    for axis, dim in sides:
        count = lax.axis_size(axis)
        forward = [(i, i + 1) for i in range(count - 1)]
        backward = [(target, source) for source, target in forward]
        low = lax.ppermute(
            lax.slice_in_dim(block, block.shape[dim] - width, None, axis=dim), axis, forward
        )
        high = lax.ppermute(lax.slice_in_dim(block, 0, width, axis=dim), axis, backward)
        block = jnp.concatenate([low, block, high], axis=dim)
    return block


def sweep_once(padded, center, rate_grid):
    laplace = (
        padded[:, :, 2:]
        + padded[:, :, :-2]
        + jnp.roll(center, 1, axis=3)
        + jnp.roll(center, -1, axis=3)
        - 4.0 * center
    )
    return center + rate_grid * laplace


def diffuse(field_now, diff_rate, step_counts):
    rate_grid = diff_rate[None, :, None, None]
    active_all = step_counts[None, :, None, None]
    for sweep_index in range(NSTEP):
        padded = extended(field_now, (("dom", 2),), 1)
        updated = sweep_once(padded, field_now, rate_grid)
        field_now = jnp.where(sweep_index < active_all, updated, field_now)
    return field_now


def from_blocks(blocks, strip_rows, lon_cells):
    leading, dom_count = (blocks.shape[0], blocks.shape[1])
    block_lon = lon_cells // dom_count
    return (
        blocks.reshape(leading, dom_count, strip_rows, block_lon)
        .transpose(0, 2, 1, 3)
        .reshape(leading, strip_rows, lon_cells)
    )


def per_device(pert_fcst, control, departures, obs_weight, diff_rate, step_counts):
    members_dev, levels, variables = (pert_fcst.shape[0], pert_fcst.shape[1], pert_fcst.shape[2])
    strip_rows, lon_cells = (control.shape[2], control.shape[3])
    dom_count = lax.axis_size("dom")
    member_count = members_dev * lax.axis_size("grp")
    factor = 1.0 / math.sqrt(member_count - 1)
    localized = diffuse(control, diff_rate, step_counts)
    received = lax.all_to_all(
        pert_fcst.reshape(members_dev * levels * variables, dom_count, -1),
        "dom",
        split_axis=1,
        concat_axis=1,
        tiled=True,
    )
    perturb = from_blocks(received, strip_rows, lon_cells).reshape(
        members_dev, levels, variables, strip_rows, lon_cells
    )
    partial_sum = jnp.sum(perturb.astype(jnp.float32) * localized[:, :, None], axis=0)
    increment = lax.psum(partial_sum, "grp") * factor
    residual = obs_weight * (increment - departures)
    adjoint = jnp.sum(perturb.astype(jnp.float32) * residual[None], axis=2) * factor
    gradient = control + diffuse(adjoint, diff_rate, step_counts)
    return (increment, gradient)


def solution(mesh):
    in_specs = (
        P("grp", None, None, "dom", None),
        P("grp", None, "dom", None),
        P(None, None, "dom", None),
        P(None, None, "dom", None),
        P(),
        P(),
    )
    out_specs = (P(None, None, "dom", None), P("grp", None, "dom", None))
    return jax.shard_map(
        per_device, mesh=mesh, in_specs=in_specs, out_specs=out_specs, check_vma=False
    )
```

profile of v0, /device:TPU:1, one launch (start us, length us, event | category | flops | bytes accessed | tf_op | source)
XLA Modules:
  0.0 297.2 jit_solution(7357680550387042396)
XLA Ops:
  7.2 1.4 reshape.23
  8.6 0.3 copy.15
  8.9 1.0 reshape.26
  9.9 23.5 %all-to-all-start = ((bf16[64,2,1024]{2,1,0:T(2,128)(2,1)}), bf16[64,2,1024]{2,1,0:T(2,128)(2,1)S(1)}, u32[]{:S(2)}, u32[]{:S(2)}) async-start(bf16[64,2,1024]{2,1,0:T(2,128)(2,1)} %reshape.26), calls=%async_computation | async-start | bytes 524288 | tf_op jit(solution)/shard_map/all_to_all | solution.py:62
  33.5 1.2 fusion.64
  34.7 4.4 %collective-permute-start.1 = (f32[2,8,1,1024]{3,2,1,0:T(1,128)S(1)}, f32[2,8,1,1024]{3,2,1,0:T(1,128)S(1)}, u32[]{:S(2)}, u32[]{:S(2)}) collective-permute-start(f32[2,8,1,1024]{3,2,1,0:T(1,128)S(1)} %get-tuple-element.51), channel_id=1, source_target_pairs={{0,1},{1,2},{2,3},{3,4},{4,5},{5,6},{6,7},{7,8},{8,9},{9,10},{10,1... | collective-permute-start | bytes 196616 | tf_op jit(solution)/shard_map/ppermute | solution.py:16
  39.1 1.9 collective-permute-start
  41.1 1.2 fusion.62
  42.4 4.2 %collective-permute-done = f32[2,8,1,1024]{3,2,1,0:T(1,128)S(1)} collective-permute-done((f32[2,8,1,1024]{3,2,1,0:T(1,128)S(1)}, f32[2,8,1,1024]{3,2,1,0:T(1,128)S(1)}, u32[]{:S(2)}, u32[]{:S(2)}) %collective-permute-start) | collective-permute-done | bytes 65568 | tf_op jit(solution)/shard_map/ppermute | solution.py:19
  46.6 0.5 add_select_fusion.7
  47.4 1.9 collective-permute-start.3
  49.3 2.4 collective-permute-start.2
  51.8 5.4 %collective-permute-done.2 = f32[2,8,1,1024]{3,2,1,0:T(1,128)S(1)} collective-permute-done((f32[2,8,1,1024]{3,2,1,0:T(1,128)S(1)}, f32[2,8,1,1024]{3,2,1,0:T(1,128)S(1)}, u32[]{:S(2)}, u32[]{:S(2)}) %collective-permute-start.2) | collective-permute-done | bytes 65568 | tf_op jit(solution)/shard_map/ppermute | solution.py:19
  57.2 0.5 add_select_fusion.6
  58.0 1.9 collective-permute-start.5
  59.9 2.4 collective-permute-start.4
  62.4 5.2 %collective-permute-done.4 = f32[2,8,1,1024]{3,2,1,0:T(1,128)S(1)} collective-permute-done((f32[2,8,1,1024]{3,2,1,0:T(1,128)S(1)}, f32[2,8,1,1024]{3,2,1,0:T(1,128)S(1)}, u32[]{:S(2)}, u32[]{:S(2)}) %collective-permute-start.4) | collective-permute-done | bytes 65568 | tf_op jit(solution)/shard_map/ppermute | solution.py:19
  67.6 0.5 add_select_fusion.5
  68.1 0.2 fusion.53
  68.4 1.9 collective-permute-start.7
  70.3 2.4 collective-permute-start.6
  72.8 5.2 %collective-permute-done.6 = f32[2,8,1,1024]{3,2,1,0:T(1,128)S(1)} collective-permute-done((f32[2,8,1,1024]{3,2,1,0:T(1,128)S(1)}, f32[2,8,1,1024]{3,2,1,0:T(1,128)S(1)}, u32[]{:S(2)}, u32[]{:S(2)}) %collective-permute-start.6) | collective-permute-done | bytes 65568 | tf_op jit(solution)/shard_map/ppermute | solution.py:19
  78.0 0.5 add_select_fusion.4
  78.5 0.3 reshape.27
  78.8 0.6 copy.12
  79.6 2.7 copy.13
  82.3 3.9 %reshape.24 = f32[2,8,2,4,1024]{4,3,2,1,0:T(4,128)S(1)} reshape(f32[32,4,64,16]{3,2,1,0:T(8,128)} %copy.13) | data formatting | bytes 1048576 | tf_op jit(solution)/shard_map/convert_element_type | solution.py:72
  86.2 0.9 multiply_reduce_fusion.1
  87.1 143.3 %all-reduce.2.cloned.1.call-done = f32[8,2,4,1024]{3,2,1,0:T(4,128)} async-done(((f32[8,2,4,1024]{3,2,1,0:T(4,128)}), f32[8,2,4,1024]{3,2,1,0:T(4,128)}) %all-reduce.2.cloned.1.call-update) | async-done | bytes 262160 | tf_op jit(solution)/shard_map/psum | solution.py:73
  230.4 1.8 subtract_multiply_fusion
  232.2 0.2 multiply_reduce_fusion
  232.6 0.2 fusion.50
  232.8 15.6 %collective-permute-start.9 = (f32[2,8,1,1024]{3,2,1,0:T(1,128)S(1)}, f32[2,8,1,1024]{3,2,1,0:T(1,128)S(1)}, u32[]{:S(2)}, u32[]{:S(2)}) collective-permute-start(f32[2,8,1,1024]{3,2,1,0:T(1,128)S(1)} %get-tuple-element.27), channel_id=1, source_target_pairs={{0,1},{1,2},{2,3},{3,4},{4,5},{5,6},{6,7},{7,8},{8,9},{9,10},{10,1... | collective-permute-start | bytes 196616 | tf_op jit(solution)/shard_map/ppermute | solution.py:16
  248.4 1.9 collective-permute-start.8
  250.4 4.5 %collective-permute-done.8 = f32[2,8,1,1024]{3,2,1,0:T(1,128)S(1)} collective-permute-done((f32[2,8,1,1024]{3,2,1,0:T(1,128)S(1)}, f32[2,8,1,1024]{3,2,1,0:T(1,128)S(1)}, u32[]{:S(2)}, u32[]{:S(2)}) %collective-permute-start.8) | collective-permute-done | bytes 65568 | tf_op jit(solution)/shard_map/ppermute | solution.py:19
  254.9 0.5 add_select_fusion.3
  255.7 2.5 collective-permute-start.11
  258.1 1.9 collective-permute-start.10
  260.1 8.5 %collective-permute-done.10 = f32[2,8,1,1024]{3,2,1,0:T(1,128)S(1)} collective-permute-done((f32[2,8,1,1024]{3,2,1,0:T(1,128)S(1)}, f32[2,8,1,1024]{3,2,1,0:T(1,128)S(1)}, u32[]{:S(2)}, u32[]{:S(2)}) %collective-permute-start.10) | collective-permute-done | bytes 65568 | tf_op jit(solution)/shard_map/ppermute | solution.py:19
  268.6 0.5 add_select_fusion.2
  269.4 1.9 collective-permute-start.13
  271.3 2.4 collective-permute-start.12
  273.8 5.0 %collective-permute-done.12 = f32[2,8,1,1024]{3,2,1,0:T(1,128)S(1)} collective-permute-done((f32[2,8,1,1024]{3,2,1,0:T(1,128)S(1)}, f32[2,8,1,1024]{3,2,1,0:T(1,128)S(1)}, u32[]{:S(2)}, u32[]{:S(2)}) %collective-permute-start.12) | collective-permute-done | bytes 65568 | tf_op jit(solution)/shard_map/ppermute | solution.py:19
  278.8 0.5 add_select_fusion.1
  279.5 1.9 collective-permute-start.15
  281.5 2.4 collective-permute-start.14
  284.0 5.2 %collective-permute-done.14 = f32[2,8,1,1024]{3,2,1,0:T(1,128)S(1)} collective-permute-done((f32[2,8,1,1024]{3,2,1,0:T(1,128)S(1)}, f32[2,8,1,1024]{3,2,1,0:T(1,128)S(1)}, u32[]{:S(2)}, u32[]{:S(2)}) %collective-permute-start.14) | collective-permute-done | bytes 65568 | tf_op jit(solution)/shard_map/ppermute | solution.py:19
  289.2 1.2 fusion
  (44 shorter events, 2.7 us)
Async XLA Ops:
  7.2 35.1 %copy-start = (f32[2,8,4,1024]{3,2,1,0:T(4,128)S(1)}, f32[2,8,4,1024]{3,2,1,0:T(4,128)}, u32[]{:S(2)}) copy-start(f32[2,8,4,1024]{3,2,1,0:T(4,128)} %param.7) | copy-start | bytes 786436
  7.2 35.2 %copy-start.4 = (s32[8]{0:T(128)S(1)}, s32[8]{0:T(128)}, u32[]{:S(2)}) copy-start(s32[8]{0:T(128)} %param.11) | copy-start | bytes 100
  7.2 39.4 %copy-start.3 = (f32[8]{0:T(128)S(1)}, f32[8]{0:T(128)}, u32[]{:S(2)}) copy-start(f32[8]{0:T(128)} %param.10) | copy-start | bytes 100
  9.9 68.6 %all-to-all-start = ((bf16[64,2,1024]{2,1,0:T(2,128)(2,1)}), bf16[64,2,1024]{2,1,0:T(2,128)(2,1)S(1)}, u32[]{:S(2)}, u32[]{:S(2)}) async-start(bf16[64,2,1024]{2,1,0:T(2,128)(2,1)} %reshape.26), calls=%async_computation | async-start | bytes 524288 | tf_op jit(solution)/shard_map/all_to_all | solution.py:62
  33.5 196.9 %all-reduce.2.cloned.1.call-start = ((), (), s32[]{:S(2)}) async-start(), calls=%async_computation.1 | async-start | bytes 524288 | tf_op jit(solution)/shard_map/psum | solution.py:73
  34.7 7.7 %collective-permute-start.1 = (f32[2,8,1,1024]{3,2,1,0:T(1,128)S(1)}, f32[2,8,1,1024]{3,2,1,0:T(1,128)S(1)}, u32[]{:S(2)}, u32[]{:S(2)}) collective-permute-start(f32[2,8,1,1024]{3,2,1,0:T(1,128)S(1)} %get-tuple-element.51), channel_id=1, source_target_pairs={{0,1},{1,2},{2,3},{3,4},{4,5},{5,6},{6,7},{7,8},{8,9},{9,10},{10,1... | collective-permute-start | bytes 196616 | tf_op jit(solution)/shard_map/ppermute | solution.py:16
  39.1 7.5 %collective-permute-start = (f32[2,8,1,1024]{3,2,1,0:T(1,128)S(1)}, f32[2,8,1,1024]{3,2,1,0:T(1,128)S(1)}, u32[]{:S(2)}, u32[]{:S(2)}) collective-permute-start(f32[2,8,1,1024]{3,2,1,0:T(1,128)S(1)} %get-tuple-element.50), channel_id=1, source_target_pairs={{1,0},{2,1},{3,2},{4,3},{5,4},{6,5},{7,6},{8,7},{9,8},{10,9},{11,1... | collective-permute-start | bytes 196616 | tf_op jit(solution)/shard_map/ppermute | solution.py:19
  47.4 4.4 %collective-permute-start.3 = (f32[2,8,1,1024]{3,2,1,0:T(1,128)S(1)}, f32[2,8,1,1024]{3,2,1,0:T(1,128)S(1)}, u32[]{:S(2)}, u32[]{:S(2)}) collective-permute-start(f32[2,8,1,1024]{3,2,1,0:T(1,128)S(1)} %get-tuple-element.45), channel_id=1, source_target_pairs={{0,1},{1,2},{2,3},{3,4},{4,5},{5,6},{6,7},{7,8},{8,9},{9,10},{10,1... | collective-permute-start | bytes 196616 | tf_op jit(solution)/shard_map/ppermute | solution.py:16
  49.3 7.9 %collective-permute-start.2 = (f32[2,8,1,1024]{3,2,1,0:T(1,128)S(1)}, f32[2,8,1,1024]{3,2,1,0:T(1,128)S(1)}, u32[]{:S(2)}, u32[]{:S(2)}) collective-permute-start(f32[2,8,1,1024]{3,2,1,0:T(1,128)S(1)} %get-tuple-element.44), channel_id=1, source_target_pairs={{1,0},{2,1},{3,2},{4,3},{5,4},{6,5},{7,6},{8,7},{9,8},{10,9},{11,1... | collective-permute-start | bytes 196616 | tf_op jit(solution)/shard_map/ppermute | solution.py:19
  58.0 4.4 %collective-permute-start.5 = (f32[2,8,1,1024]{3,2,1,0:T(1,128)S(1)}, f32[2,8,1,1024]{3,2,1,0:T(1,128)S(1)}, u32[]{:S(2)}, u32[]{:S(2)}) collective-permute-start(f32[2,8,1,1024]{3,2,1,0:T(1,128)S(1)} %get-tuple-element.39), channel_id=1, source_target_pairs={{0,1},{1,2},{2,3},{3,4},{4,5},{5,6},{6,7},{7,8},{8,9},{9,10},{10,1... | collective-permute-start | bytes 196616 | tf_op jit(solution)/shard_map/ppermute | solution.py:16
  59.9 7.7 %collective-permute-start.4 = (f32[2,8,1,1024]{3,2,1,0:T(1,128)S(1)}, f32[2,8,1,1024]{3,2,1,0:T(1,128)S(1)}, u32[]{:S(2)}, u32[]{:S(2)}) collective-permute-start(f32[2,8,1,1024]{3,2,1,0:T(1,128)S(1)} %get-tuple-element.38), channel_id=1, source_target_pairs={{1,0},{2,1},{3,2},{4,3},{5,4},{6,5},{7,6},{8,7},{9,8},{10,9},{11,1... | collective-permute-start | bytes 196616 | tf_op jit(solution)/shard_map/ppermute | solution.py:19
  68.4 4.4 %collective-permute-start.7 = (f32[2,8,1,1024]{3,2,1,0:T(1,128)S(1)}, f32[2,8,1,1024]{3,2,1,0:T(1,128)S(1)}, u32[]{:S(2)}, u32[]{:S(2)}) collective-permute-start(f32[2,8,1,1024]{3,2,1,0:T(1,128)S(1)} %get-tuple-element.33), channel_id=1, source_target_pairs={{0,1},{1,2},{2,3},{3,4},{4,5},{5,6},{6,7},{7,8},{8,9},{9,10},{10,1... | collective-permute-start | bytes 196616 | tf_op jit(solution)/shard_map/ppermute | solution.py:16
  70.3 7.7 %collective-permute-start.6 = (f32[2,8,1,1024]{3,2,1,0:T(1,128)S(1)}, f32[2,8,1,1024]{3,2,1,0:T(1,128)S(1)}, u32[]{:S(2)}, u32[]{:S(2)}) collective-permute-start(f32[2,8,1,1024]{3,2,1,0:T(1,128)S(1)} %get-tuple-element.32), channel_id=1, source_target_pairs={{1,0},{2,1},{3,2},{4,3},{5,4},{6,5},{7,6},{8,7},{9,8},{10,9},{11,1... | collective-permute-start | bytes 196616 | tf_op jit(solution)/shard_map/ppermute | solution.py:19
  82.3 148.1 %copy-start.1 = (f32[8,2,4,1024]{3,2,1,0:T(4,128)S(1)}, f32[8,2,4,1024]{3,2,1,0:T(4,128)}, u32[]{:S(2)}) copy-start(f32[8,2,4,1024]{3,2,1,0:T(4,128)} %param.9) | copy-start | bytes 786436
  82.3 148.1 %copy-start.2 = (f32[8,2,4,1024]{3,2,1,0:T(4,128)S(1)}, f32[8,2,4,1024]{3,2,1,0:T(4,128)}, u32[]{:S(2)}) copy-start(f32[8,2,4,1024]{3,2,1,0:T(4,128)} %param.8) | copy-start | bytes 786436
  232.8 17.6 %collective-permute-start.9 = (f32[2,8,1,1024]{3,2,1,0:T(1,128)S(1)}, f32[2,8,1,1024]{3,2,1,0:T(1,128)S(1)}, u32[]{:S(2)}, u32[]{:S(2)}) collective-permute-start(f32[2,8,1,1024]{3,2,1,0:T(1,128)S(1)} %get-tuple-element.27), channel_id=1, source_target_pairs={{0,1},{1,2},{2,3},{3,4},{4,5},{5,6},{6,7},{7,8},{8,9},{9,10},{10,1... | collective-permute-start | bytes 196616 | tf_op jit(solution)/shard_map/ppermute | solution.py:16
  248.4 6.5 %collective-permute-start.8 = (f32[2,8,1,1024]{3,2,1,0:T(1,128)S(1)}, f32[2,8,1,1024]{3,2,1,0:T(1,128)S(1)}, u32[]{:S(2)}, u32[]{:S(2)}) collective-permute-start(f32[2,8,1,1024]{3,2,1,0:T(1,128)S(1)} %get-tuple-element.26), channel_id=1, source_target_pairs={{1,0},{2,1},{3,2},{4,3},{5,4},{6,5},{7,6},{8,7},{9,8},{10,9},{11,1... | collective-permute-start | bytes 196616 | tf_op jit(solution)/shard_map/ppermute | solution.py:19
  255.7 4.5 %collective-permute-start.11 = (f32[2,8,1,1024]{3,2,1,0:T(1,128)S(1)}, f32[2,8,1,1024]{3,2,1,0:T(1,128)S(1)}, u32[]{:S(2)}, u32[]{:S(2)}) collective-permute-start(f32[2,8,1,1024]{3,2,1,0:T(1,128)S(1)} %get-tuple-element.21), channel_id=1, source_target_pairs={{0,1},{1,2},{2,3},{3,4},{4,5},{5,6},{6,7},{7,8},{8,9},{9,10},{10,1... | collective-permute-start | bytes 196616 | tf_op jit(solution)/shard_map/ppermute | solution.py:16
  258.1 10.5 %collective-permute-start.10 = (f32[2,8,1,1024]{3,2,1,0:T(1,128)S(1)}, f32[2,8,1,1024]{3,2,1,0:T(1,128)S(1)}, u32[]{:S(2)}, u32[]{:S(2)}) collective-permute-start(f32[2,8,1,1024]{3,2,1,0:T(1,128)S(1)} %get-tuple-element.20), channel_id=1, source_target_pairs={{1,0},{2,1},{3,2},{4,3},{5,4},{6,5},{7,6},{8,7},{9,8},{10,9},{11,1... | collective-permute-start | bytes 196616 | tf_op jit(solution)/shard_map/ppermute | solution.py:19
  269.4 4.4 %collective-permute-start.13 = (f32[2,8,1,1024]{3,2,1,0:T(1,128)S(1)}, f32[2,8,1,1024]{3,2,1,0:T(1,128)S(1)}, u32[]{:S(2)}, u32[]{:S(2)}) collective-permute-start(f32[2,8,1,1024]{3,2,1,0:T(1,128)S(1)} %get-tuple-element.15), channel_id=1, source_target_pairs={{0,1},{1,2},{2,3},{3,4},{4,5},{5,6},{6,7},{7,8},{8,9},{9,10},{10,1... | collective-permute-start | bytes 196616 | tf_op jit(solution)/shard_map/ppermute | solution.py:16
  271.3 7.5 %collective-permute-start.12 = (f32[2,8,1,1024]{3,2,1,0:T(1,128)S(1)}, f32[2,8,1,1024]{3,2,1,0:T(1,128)S(1)}, u32[]{:S(2)}, u32[]{:S(2)}) collective-permute-start(f32[2,8,1,1024]{3,2,1,0:T(1,128)S(1)} %get-tuple-element.14), channel_id=1, source_target_pairs={{1,0},{2,1},{3,2},{4,3},{5,4},{6,5},{7,6},{8,7},{9,8},{10,9},{11,1... | collective-permute-start | bytes 196616 | tf_op jit(solution)/shard_map/ppermute | solution.py:19
  279.5 4.4 %collective-permute-start.15 = (f32[2,8,1,1024]{3,2,1,0:T(1,128)S(1)}, f32[2,8,1,1024]{3,2,1,0:T(1,128)S(1)}, u32[]{:S(2)}, u32[]{:S(2)}) collective-permute-start(f32[2,8,1,1024]{3,2,1,0:T(1,128)S(1)} %get-tuple-element.9), channel_id=1, source_target_pairs={{0,1},{1,2},{2,3},{3,4},{4,5},{5,6},{6,7},{7,8},{8,9},{9,10},{10,1... | collective-permute-start | bytes 196616 | tf_op jit(solution)/shard_map/ppermute | solution.py:16
  281.5 7.7 %collective-permute-start.14 = (f32[2,8,1,1024]{3,2,1,0:T(1,128)S(1)}, f32[2,8,1,1024]{3,2,1,0:T(1,128)S(1)}, u32[]{:S(2)}, u32[]{:S(2)}) collective-permute-start(f32[2,8,1,1024]{3,2,1,0:T(1,128)S(1)} %get-tuple-element.8), channel_id=1, source_target_pairs={{1,0},{2,1},{3,2},{4,3},{5,4},{6,5},{7,6},{8,7},{9,8},{10,9},{11,1... | collective-permute-start | bytes 196616 | tf_op jit(solution)/shard_map/ppermute | solution.py:19
Sparse Core Ops, SparseCore 0:
  87.3 143.1 all-reduce.1
where the time goes:
time: 300 us; the launch traced here: 297 us
  waiting for transfers between devices  186 us (62%)
  starting transfers between devices  73.4 us (24%)
  local copies, waits for them, and re-layouts  15.5 us (5%)
  between operations  14.4 us (5%)
  other arithmetic  7.48 us (2%)
    psum x1, waiting for transfers between devices, per_device(): increment = lax.psum(partial_sum, 'grp') * factor  143 us
    ppermute x8, waiting for transfers between devices, extended(): lax.ppermute(lax.slice_in_dim(block, 0, width, axis=dim), axis, backward)  43.1 us
    ppermute x8, starting transfers between devices, extended(): lax.ppermute(lax.slice_in_dim(block, block.shape[dim] - width, None, axis...  32 us
    all_to_all x1, starting transfers between devices, per_device(): lax.all_to_all(pert_fcst.reshape(members_dev * levels * variables, dom_co...  23.5 us
    ppermute x8, starting transfers between devices, extended(): lax.ppermute(lax.slice_in_dim(block, 0, width, axis=dim), axis, backward)  17.8 us
    convert_element_type x2, local copies, waits for them, and re-layouts, per_device(): perturb.astype(jnp.float32) * localized[:, :, None]  6.59 us
  transfers between devices with their start and end apart: 18, of which 9 were waited for; matrix products, arithmetic and copies ran while one was open for 2% of the time, Pallas kernels for 0%

commit v1 on v0

v1 whole, which is shorter than its diff:
```python
import functools
import math

import jax
import jax.numpy as jnp
from jax import lax
from jax.experimental import pallas as pl
from jax.experimental.pallas import tpu as pltpu
from jax.sharding import PartitionSpec as P

NSTEP = 4
MEM = 2
LEV = 8
VAR = 2
ROWS = 4
LON = 1024
LANES = 128
TILES = LON // LANES
SLOT = 16
HALF = LON // 2
NDOM = 64
NGRP = 16
MESH = pl.DeviceIdType.MESH


def lane_iota(shape):
    return lax.broadcasted_iota(jnp.int32, shape, len(shape) - 1)


def remote(src, dst, send_sem, recv_sem, device):
    return pltpu.make_async_remote_copy(
        src_ref=src,
        dst_ref=dst,
        send_sem=send_sem,
        recv_sem=recv_sem,
        device_id=device,
        device_id_type=MESH,
    )


def wait_bytes(ref, sem):
    pltpu.make_async_copy(ref, ref, sem).wait()


def wide(tile):
    return jnp.concatenate([tile] * TILES, axis=1)


def sweeps(src, other, coef, m, emit):
    bufs = (src, other)
    for s in range(NSTEP):
        old, new = bufs[s % 2], bufs[(s + 1) % 2]
        first, last = s + 1, 3 * ROWS - 1 - s
        north = old[m, first - 1]
        here = old[m, first]
        for row in range(first, last):
            south = old[m, row + 1]
            which = 0 if ROWS <= row < 2 * ROWS else (1 if row < ROWS else 2)
            rate = wide(coef[3 * s + which])
            lap = (
                north
                + south
                + pltpu.roll(here, 1, axis=1)
                + pltpu.roll(here, LON - 1, axis=1)
                - 4.0 * here
            )
            value = here + rate * lap
            if s == NSTEP - 1:
                emit(row - ROWS, value)
            else:
                new[m, row] = value
            north, here = here, south


def kernel(
    factor,
    rate_ref,
    steps_ref,
    pert_ref,
    ctl_ref,
    dep_ref,
    wgt_ref,
    inc_ref,
    grad_ref,
    pf,
    packed,
    got,
    pert,
    up_raw,
    dn_raw,
    ext,
    tmp,
    ext2,
    loc,
    coef,
    part,
    red,
    incs,
    a2a_send,
    a2a_recv,
    halo_send,
    halo_recv,
    rs_send,
    rs_recv,
    ag_send,
    ag_recv,
    adj_send,
    adj_recv,
):
    g = lax.axis_index("grp")
    d = lax.axis_index("dom")
    below = lax.rem(d + 1, NDOM)
    above = lax.rem(d + NDOM - 1, NDOM)

    barrier = pltpu.get_barrier_semaphore()

    def greet_dom(k, carry):
        pl.semaphore_signal(
            barrier, inc=1, device_id=(g, lax.rem(d + k, NDOM)), device_id_type=MESH
        )
        return carry

    def greet_grp(k, carry):
        pl.semaphore_signal(
            barrier, inc=1, device_id=(lax.rem(g + k, NGRP), d), device_id_type=MESH
        )
        return carry

    lax.fori_loop(1, NDOM, greet_dom, 0)
    lax.fori_loop(1, NGRP, greet_grp, 0)

    pf[...] = pert_ref[...].astype(jnp.float32)
    low = lane_iota((LEV, LANES)) < 64

    def pack(q, carry):
        firsts, seconds = [], []
        for v in range(VAR):
            a = pf[pl.ds(q * 2 + v, LEV, stride=64), :]
            b = pf[pl.ds(512 + q * 2 + v, LEV, stride=64), :]
            firsts.append(jnp.where(low, a, pltpu.roll(b, 64, axis=1)))
            seconds.append(jnp.where(low, pltpu.roll(a, 64, axis=1), b))
        packed[2 * q] = jnp.concatenate(firsts, axis=0).astype(jnp.bfloat16)
        packed[2 * q + 1] = jnp.concatenate(seconds, axis=0).astype(jnp.bfloat16)
        return carry

    lax.fori_loop(0, NDOM // 2, pack, 0)

    level = lax.broadcasted_iota(jnp.int32, (LEV, LANES), 0)
    rate = jnp.zeros((LEV, LANES), jnp.float32)
    count = jnp.zeros((LEV, LANES), jnp.int32)
    for l in range(LEV):
        rate = jnp.where(level == l, rate_ref[l], rate)
        count = jnp.where(level == l, steps_ref[l], count)
    has_up = jnp.where(d > 0, 1.0, 0.0).astype(jnp.float32)
    has_dn = jnp.where(d < NDOM - 1, 1.0, 0.0).astype(jnp.float32)
    for s in range(NSTEP):
        now = jnp.where(s < count, rate, 0.0)
        coef[3 * s] = now
        coef[3 * s + 1] = now * has_up
        coef[3 * s + 2] = now * has_dn

    pl.semaphore_wait(barrier, NDOM - 1 + NGRP - 1)

    to_below = remote(ctl_ref, up_raw, halo_send.at[0], halo_recv.at[0], (g, below))
    to_above = remote(ctl_ref, dn_raw, halo_send.at[1], halo_recv.at[1], (g, above))
    to_below.start()
    to_above.start()

    def send_tile(k):
        to = lax.rem(d + k, NDOM)
        remote(packed.at[to], got.at[d], a2a_send, a2a_recv, (g, to)).start()

    send_tile(NDOM // 2)

    def send_pair(j, carry):
        send_tile(NDOM // 2 - j)
        send_tile(NDOM // 2 + j)
        return carry

    lax.fori_loop(1, NDOM // 2, send_pair, 0)
    got[d] = packed[d]

    def fill(source, base_row):
        def body(n, carry):
            m, i = n // ROWS, lax.rem(n, ROWS)
            for t in range(TILES):
                ext[m, base_row + i, :, t * LANES : (t + 1) * LANES] = source[
                    pl.ds(m * 256 + t * ROWS + i, LEV, stride=32), :
                ]
            return carry

        lax.fori_loop(0, MEM * ROWS, body, 0)

    def clear(buffer, base_row):
        for m in range(MEM):
            for i in range(ROWS):
                buffer[m, base_row + i] = jnp.zeros((LEV, LON), jnp.float32)

    fill(ctl_ref, ROWS)
    to_below.wait_recv()
    to_above.wait_recv()
    fill(up_raw, 0)
    fill(dn_raw, 2 * ROWS)

    @pl.when(d == 0)
    def _():
        clear(ext, 0)

    @pl.when(d == NDOM - 1)
    def _():
        clear(ext, 2 * ROWS)

    def localize(m, carry):
        def emit(i, value):
            loc[m * ROWS + i] = value

        sweeps(ext, tmp, coef, m, emit)
        return carry

    lax.fori_loop(0, MEM, localize, 0)

    wait_bytes(got.at[pl.ds(0, NDOM - 1)], a2a_recv)
    slot = lane_iota((2 * LEV, LANES)) // SLOT

    def relayout(t, carry):
        tiles = [got[t * TILES + c].astype(jnp.float32) for c in range(TILES)]
        for step in (4, 2, 1):
            high = (slot & step) != 0
            for a in range(TILES):
                if a & step:
                    continue
                x, y = tiles[a], tiles[a + step]
                tiles[a] = jnp.where(high, pltpu.roll(y, step * SLOT, axis=1), x)
                tiles[a + step] = jnp.where(
                    high, y, pltpu.roll(x, LANES - step * SLOT, axis=1)
                )
        for k in range(TILES):
            pert[k, :, pl.ds(pl.multiple_of(t * LANES, LANES), LANES)] = tiles[k]
        return carry

    lax.fori_loop(0, TILES, relayout, 0)

    def share(n, carry):
        i, h = n // 2, lax.rem(n, 2)
        cols = pl.ds(pl.multiple_of(h * HALF, HALF), HALF)
        for v in range(VAR):
            rows = slice(v * LEV, (v + 1) * LEV)
            part[(v * ROWS + i) * 2 + h] = (
                pert[i, rows, cols] * loc[i, :, cols]
                + pert[ROWS + i, rows, cols] * loc[ROWS + i, :, cols]
            )
        return carry

    lax.fori_loop(0, 2 * ROWS, share, 0)

    def scatter(k, carry):
        to = lax.rem(g + k, NGRP)
        remote(part.at[to], red.at[g], rs_send, rs_recv, (to, d)).start()
        return carry

    lax.fori_loop(1, NGRP, scatter, 0)
    red[g] = part[g]
    wait_bytes(red.at[pl.ds(0, NGRP - 1)], rs_recv)
    total = red[0]
    for n in range(1, NGRP):
        total = total + red[n]
    incs[g] = total * factor

    def gather(k, carry):
        to = lax.rem(g + k, NGRP)
        remote(incs.at[g], incs.at[g], ag_send, ag_recv, (to, d)).start()
        return carry

    lax.fori_loop(1, NGRP, gather, 0)
    wait_bytes(incs.at[pl.ds(0, NGRP - 1)], ag_recv)

    def back(i, carry):
        for h in range(2):
            for c in range(TILES // 2):
                t = h * (TILES // 2) + c
                cols = slice(t * LANES, (t + 1) * LANES)
                res = []
                for v in range(VAR):
                    lines = pl.ds(v * 32 + t * ROWS + i, LEV, stride=64)
                    inc = incs[(v * ROWS + i) * 2 + h, :, c * LANES : (c + 1) * LANES]
                    inc_ref[lines, :] = inc
                    res.append(wgt_ref[lines, :] * (inc - dep_ref[lines, :]))
                for m in range(MEM):
                    ext2[m, ROWS + i, :, cols] = (
                        pert[m * ROWS + i, 0:LEV, cols] * res[0]
                        + pert[m * ROWS + i, LEV : 2 * LEV, cols] * res[1]
                    ) * factor
        return carry

    lax.fori_loop(0, ROWS, back, 0)

    def adj_copies(m):
        own = ext2.at[m, pl.ds(ROWS, ROWS)]
        return (
            remote(own, ext2.at[m, pl.ds(0, ROWS)], adj_send.at[m], adj_recv.at[m], (g, below)),
            remote(
                own,
                ext2.at[m, pl.ds(2 * ROWS, ROWS)],
                adj_send.at[2 + m],
                adj_recv.at[2 + m],
                (g, above),
            ),
        )

    copies = [c for m in range(MEM) for c in adj_copies(m)]
    for c in copies:
        c.start()
    for c in copies:
        c.wait_recv()

    @pl.when(d == 0)
    def _():
        clear(ext2, 0)

    @pl.when(d == NDOM - 1)
    def _():
        clear(ext2, 2 * ROWS)

    def gradient(m, carry):
        def emit(i, value):
            for t in range(TILES):
                lines = pl.ds(m * 256 + t * ROWS + i, LEV, stride=32)
                grad_ref[lines, :] = ctl_ref[lines, :] + value[:, t * LANES : (t + 1) * LANES]

        sweeps(ext2, tmp, coef, m, emit)
        return carry

    for c in copies:
        c.wait_send()
    lax.fori_loop(0, MEM, gradient, 0)

    to_below.wait_send()
    to_above.wait_send()
    wait_bytes(packed.at[pl.ds(0, NDOM - 1)], a2a_send)
    wait_bytes(part.at[pl.ds(0, NGRP - 1)], rs_send)
    wait_bytes(incs.at[pl.ds(0, NGRP - 1)], ag_send)


def tiles_of(x):
    a, b, rows, lon = x.shape
    return (
        x.reshape(a, b, rows, lon // LANES, LANES)
        .transpose(0, 1, 3, 2, 4)
        .reshape(a * b * rows * lon // LANES, LANES)
    )


def from_tiles(x, shape):
    a, b, rows, lon = shape
    return (
        x.reshape(a, b, lon // LANES, rows, LANES).transpose(0, 1, 3, 2, 4).reshape(shape)
    )


def per_device(pert_fcst, control, departures, obs_weight, diff_rate, step_counts):
    members = MEM * lax.axis_size("grp")
    factor = 1.0 / math.sqrt(members - 1)
    pert = (
        pert_fcst.reshape(MEM, LEV, VAR, 32, LANES)
        .transpose(0, 1, 3, 2, 4)
        .reshape(MEM * LEV * 32 * VAR, LANES)
    )
    vmem = pl.BlockSpec(memory_space=pltpu.VMEM)
    smem = pl.BlockSpec(memory_space=pltpu.SMEM)
    flat = (MEM * LEV * ROWS * TILES, LANES)
    f32 = jnp.float32
    dma = pltpu.SemaphoreType.DMA
    inc, grad = pl.pallas_call(
        functools.partial(kernel, factor),
        out_shape=(jax.ShapeDtypeStruct(flat, f32), jax.ShapeDtypeStruct(flat, f32)),
        in_specs=[smem, smem, vmem, vmem, vmem, vmem],
        out_specs=(vmem, vmem),
        scratch_shapes=[
            pltpu.VMEM((1024, LANES), f32),
            pltpu.VMEM((NDOM, 16, LANES), jnp.bfloat16),
            pltpu.VMEM((NDOM, 16, LANES), jnp.bfloat16),
            pltpu.VMEM((MEM * ROWS, VAR * LEV, LON), f32),
            pltpu.VMEM(flat, f32),
            pltpu.VMEM(flat, f32),
            pltpu.VMEM((MEM, 3 * ROWS, LEV, LON), f32),
            pltpu.VMEM((MEM, 3 * ROWS, LEV, LON), f32),
            pltpu.VMEM((MEM, 3 * ROWS, LEV, LON), f32),
            pltpu.VMEM((MEM * ROWS, LEV, LON), f32),
            pltpu.VMEM((3 * NSTEP, LEV, LANES), f32),
            pltpu.VMEM((NGRP, LEV, HALF), f32),
            pltpu.VMEM((NGRP, LEV, HALF), f32),
            pltpu.VMEM((NGRP, LEV, HALF), f32),
            dma,
            dma,
            dma((2,)),
            dma((2,)),
            dma,
            dma,
            dma,
            dma,
            dma((4,)),
            dma((4,)),
        ],
        compiler_params=pltpu.CompilerParams(
            collective_id=0, has_side_effects=True, vmem_limit_bytes=48 * 1024 * 1024
        ),
    )(
        diff_rate,
        step_counts,
        pert,
        tiles_of(control),
        tiles_of(departures),
        tiles_of(obs_weight),
    )
    return (from_tiles(inc, (LEV, VAR, ROWS, LON)), from_tiles(grad, (MEM, LEV, ROWS, LON)))


def solution(mesh):
    in_specs = (
        P("grp", None, None, "dom", None),
        P("grp", None, "dom", None),
        P(None, None, "dom", None),
        P(None, None, "dom", None),
        P(),
        P(),
    )
    out_specs = (P(None, None, "dom", None), P("grp", None, "dom", None))
    return jax.shard_map(
        per_device, mesh=mesh, in_specs=in_specs, out_specs=out_specs, check_vma=False
    )
```

time: 300 us -> 77.6 us (0.26)
  waiting for transfers between devices: 186 us -> 0 us
  starting transfers between devices: 73.4 us -> 0 us
  Pallas kernels: 0 us -> 70.8 us
  between operations: 14.4 us -> 0.66 us
  local copies, waits for them, and re-layouts: 15.5 us -> 5.86 us
  other arithmetic: 7.48 us -> 0 us
    psum x1 -> x0, waiting for transfers between devices: 143 us -> none  [per_device(): increment = lax.psum(partial_sum, 'grp') * factor]
    pallas_call x0 -> x1, Pallas kernels: none -> 70.8 us  [per_device(): pl.pallas_call(functools.partial(kernel, factor), out_shape=(jax.ShapeDty...]
    ppermute x16 -> x0, starting transfers between devices: 49.8 us -> none  [the longest x8 32 us: extended(): lax.ppermute(lax.slice_in_dim(block, block.shape[dim] - width, None, axis...]
    ppermute x16 -> x0, waiting for transfers between devices: 43.1 us -> none  [the longest x8 43.1 us: extended(): lax.ppermute(lax.slice_in_dim(block, 0, width, axis=dim), axis, backward)]
    all_to_all x1 -> x0, starting transfers between devices: 23.5 us -> none  [per_device(): lax.all_to_all(pert_fcst.reshape(members_dev * levels * variables, dom_co...]
    convert_element_type x2 -> x0, local copies, waits for them, and re-layouts: 6.59 us -> none  [per_device(): perturb.astype(jnp.float32) * localized[:, :, None]]
    slice x24 -> x0, local copies, waits for them, and re-layouts: 5.22 us -> none  [the longest x16 3.33 us: sweep_once(): jnp.roll(center, -1, axis=3)]
    unnamed x12 -> x14, local copies, waits for them, and re-layouts: 1.37 us -> 5.86 us
  transfers between devices with their start and end apart: 18 -> 0, of which waited for: 9 -> 0; matrix products, arithmetic and copies ran while one was open for 2% -> 0% of each run, Pallas kernels for 0% -> 0%
where the time goes in v1:
time: 77.6 us; the launch traced here: 77.3 us
  Pallas kernels  70.8 us (91%)
  local copies, waits for them, and re-layouts  5.86 us (8%)
    pallas_call x1, Pallas kernels, per_device(): pl.pallas_call(functools.partial(kernel, factor), out_shape=(jax.ShapeDty...  70.8 us
    unnamed x14, local copies, waits for them, and re-layouts  5.86 us

profile of v1, /device:TPU:1, one launch (start us, length us, event | category | flops | bytes accessed | tf_op | source)
XLA Modules:
  0.0 77.3 jit_solution(8564270435146470419)
XLA Ops:
  0.6 0.0 copy-start.4
  0.6 0.0 copy-start.5
  0.7 0.6 copy-done.4
  1.3 0.0 copy-done.5
  1.3 0.0 copy-start
  1.3 0.9 %copy-done = bf16[2,8,2,1,4096]{4,2,3,1,0:T(2,128)(2,1)S(1)} copy-done((bf16[2,8,2,1,4096]{4,2,3,1,0:T(2,128)(2,1)S(1)}, bf16[2,8,2,1,4096]{4,2,3,1,0:T(2,128)(2,1)}, u32[]{:S(2)}) %copy-start) | copy-done | bytes 262168
  2.3 0.0 copy-start.1
  2.3 0.9 %copy-done.1 = f32[2,8,4,1024]{3,2,1,0:T(4,128)S(1)} copy-done((f32[2,8,4,1024]{3,2,1,0:T(4,128)S(1)}, f32[2,8,4,1024]{3,2,1,0:T(4,128)}, u32[]{:S(2)}) %copy-start.1) | copy-done | bytes 262168
  3.2 0.0 copy-start.2
  3.2 0.9 %copy-done.2 = f32[8,2,4,1024]{3,2,1,0:T(4,128)S(1)} copy-done((f32[8,2,4,1024]{3,2,1,0:T(4,128)S(1)}, f32[8,2,4,1024]{3,2,1,0:T(4,128)}, u32[]{:S(2)}) %copy-start.2) | copy-done | bytes 262168
  4.2 0.0 copy-start.3
  4.2 0.9 %copy-done.3 = f32[8,2,4,1024]{3,2,1,0:T(4,128)S(1)} copy-done((f32[8,2,4,1024]{3,2,1,0:T(4,128)S(1)}, f32[8,2,4,1024]{3,2,1,0:T(4,128)}, u32[]{:S(2)}) %copy-start.3) | copy-done | bytes 262168
  5.1 70.8 %shard_map.77 = (f32[512,128]{1,0:T(8,128)S(1)}, f32[512,128]{1,0:T(8,128)S(1)}) custom-call(f32[8]{0:T(128)S(1)} %copy-done.4, s32[8]{0:T(128)S(1)} %copy-done.5, bf16[1024,128]{1,0:T(8,128)(2,1)S(1)} %bitcast.30, f32[512,128]{1,0:T(8,128)S(1)} %bitcast.31, f32[512,128]{1,0:T(8,128)S(1)} %bitcast.32, f32[512,128]{1,0:T(8,128)S(1)} %bitcast.33), custom_call_target="tpu_custom_call" | custom-call | tf_op jit(solution)/shard_map/pallas_call | solution.py:373
  75.9 0.7 copy.16
  76.6 0.7 copy.17
Async XLA Ops:
  0.6 0.7 copy-start.4
  0.6 0.7 copy-start.5
  1.3 0.9 %copy-start = (bf16[2,8,2,1,4096]{4,2,3,1,0:T(2,128)(2,1)S(1)}, bf16[2,8,2,1,4096]{4,2,3,1,0:T(2,128)(2,1)}, u32[]{:S(2)}) copy-start(bf16[2,8,2,1,4096]{4,2,3,1,0:T(2,128)(2,1)} %param.6) | copy-start | bytes 786436
  2.3 0.9 %copy-start.1 = (f32[2,8,4,1024]{3,2,1,0:T(4,128)S(1)}, f32[2,8,4,1024]{3,2,1,0:T(4,128)}, u32[]{:S(2)}) copy-start(f32[2,8,4,1024]{3,2,1,0:T(4,128)} %param.7) | copy-start | bytes 786436
  3.2 0.9 %copy-start.2 = (f32[8,2,4,1024]{3,2,1,0:T(4,128)S(1)}, f32[8,2,4,1024]{3,2,1,0:T(4,128)}, u32[]{:S(2)}) copy-start(f32[8,2,4,1024]{3,2,1,0:T(4,128)} %param.8) | copy-start | bytes 786436
  4.2 0.9 %copy-start.3 = (f32[8,2,4,1024]{3,2,1,0:T(4,128)S(1)}, f32[8,2,4,1024]{3,2,1,0:T(4,128)}, u32[]{:S(2)}) copy-start(f32[8,2,4,1024]{3,2,1,0:T(4,128)} %param.9) | copy-start | bytes 786436

commit v2 on v1

v2 whole, which is shorter than its diff:
```python
import functools
import math

import jax
import jax.numpy as jnp
from jax import lax
from jax.experimental import pallas as pl
from jax.experimental.pallas import tpu as pltpu
from jax.sharding import PartitionSpec as P

NSTEP = 4
MEM = 2
LEV = 8
VAR = 2
ROWS = 4
LON = 1024
LANES = 128
TILES = LON // LANES
SLOT = 16
HALF = LON // 2
NDOM = 64
NGRP = 16
MESH = pl.DeviceIdType.MESH
FAR_FIRST_8 = (4, 3, 5, 2, 6, 1, 7)
FAR_FIRST_16 = (8, 7, 9, 6, 10, 5, 11, 4, 12, 3, 13, 2, 14, 1, 15)


def lane_iota(shape):
    return lax.broadcasted_iota(jnp.int32, shape, len(shape) - 1)


def remote(src, dst, send_sem, recv_sem, device):
    return pltpu.make_async_remote_copy(
        src_ref=src,
        dst_ref=dst,
        send_sem=send_sem,
        recv_sem=recv_sem,
        device_id=device,
        device_id_type=MESH,
    )


def wait_bytes(ref, sem):
    pltpu.make_async_copy(ref, ref, sem).wait()


def wide(tile):
    return jnp.concatenate([tile] * TILES, axis=1)


def sweeps(src, other, coef, m, emit):
    bufs = (src, other)
    for s in range(NSTEP):
        old, new = bufs[s % 2], bufs[(s + 1) % 2]
        first, last = s + 1, 3 * ROWS - 1 - s
        north = old[m, first - 1]
        here = old[m, first]
        for row in range(first, last):
            south = old[m, row + 1]
            which = 0 if ROWS <= row < 2 * ROWS else (1 if row < ROWS else 2)
            rate = wide(coef[3 * s + which])
            lap = (
                north
                + south
                + pltpu.roll(here, 1, axis=1)
                + pltpu.roll(here, LON - 1, axis=1)
                - 4.0 * here
            )
            value = here + rate * lap
            if s == NSTEP - 1:
                emit(row - ROWS, value)
            else:
                new[m, row] = value
            north, here = here, south


def kernel(
    factor,
    rate_hbm,
    steps_hbm,
    pert_hbm,
    ctl_hbm,
    dep_hbm,
    wgt_hbm,
    inc_ref,
    grad_ref,
    rate_ref,
    steps_ref,
    pert_ref,
    ctl_ref,
    dep_ref,
    wgt_ref,
    pf,
    packed,
    mid,
    got,
    pert,
    up_raw,
    dn_raw,
    ext,
    tmp,
    ext2,
    loc,
    coef,
    part,
    red,
    incs,
    load_sem,
    y_send,
    y_recv,
    z_send,
    z_recv,
    halo_send,
    halo_recv,
    rs_send,
    rs_recv,
    ag_send,
    ag_recv,
    adj_send,
    adj_recv,
):
    loads = [
        pltpu.make_async_copy(src, dst, load_sem.at[n])
        for n, (src, dst) in enumerate(
            (
                (pert_hbm, pert_ref),
                (ctl_hbm, ctl_ref),
                (dep_hbm, dep_ref),
                (wgt_hbm, wgt_ref),
                (rate_hbm, rate_ref),
                (steps_hbm, steps_ref),
            )
        )
    ]
    for load in loads:
        load.start()

    g = lax.axis_index("grp")
    d = lax.axis_index("dom")
    y, c = d // TILES, lax.rem(d, TILES)
    below = lax.rem(d + 1, NDOM)
    above = lax.rem(d + NDOM - 1, NDOM)

    barrier = pltpu.get_barrier_semaphore()

    def greet(to):
        pl.semaphore_signal(barrier, inc=1, device_id=to, device_id_type=MESH)

    def y_mate(k):
        return lax.rem(y + k, TILES)

    def z_mate(k):
        return lax.rem(c + k, TILES)

    for k in FAR_FIRST_8:
        greet((g, y_mate(k) * TILES + c))
        greet((g, y * TILES + z_mate(k)))
    for k in FAR_FIRST_16:
        greet((lax.rem(g + k, NGRP), d))

    @pl.when(c == TILES - 1)
    def _():
        greet((g, below))

    @pl.when(c == 0)
    def _():
        greet((g, above))

    loads[0].wait()
    pf[...] = pert_ref[...].astype(jnp.float32)
    low = lane_iota((LEV, LANES)) < 64
    for v in range(VAR):

        def pack(q, carry):
            a = pf[pl.ds(q * 2 + v, LEV, stride=64), :]
            b = pf[pl.ds(512 + q * 2 + v, LEV, stride=64), :]
            first = jnp.where(low, a, pltpu.roll(b, 64, axis=1))
            second = jnp.where(low, pltpu.roll(a, 64, axis=1), b)
            to_y, to_c = q // 4, 2 * lax.rem(q, 4)
            packed[v, to_y, to_c] = first.astype(jnp.bfloat16)
            packed[v, to_y, to_c + 1] = second.astype(jnp.bfloat16)
            return carry

        lax.fori_loop(0, NDOM // 2, pack, 0, unroll=4)

    loads[1].wait()
    ends = c // (TILES - 1) + (TILES - 1 - c) // (TILES - 1)
    pl.semaphore_wait(barrier, 2 * (TILES - 1) + NGRP - 1 + ends)

    def send_y(v):
        for k in FAR_FIRST_8:
            to = y_mate(k)
            remote(
                packed.at[v, to], mid.at[v, y], y_send.at[v], y_recv.at[v], (g, to * TILES + c)
            ).start()

    def send_z(v):
        wait_bytes(mid.at[v, pl.ds(0, TILES - 1)], y_recv.at[v])
        for k in FAR_FIRST_8:
            to = z_mate(k)
            remote(
                mid.at[v, :, to],
                got.at[v, :, c],
                z_send.at[v],
                z_recv.at[v],
                (g, y * TILES + to),
            ).start()
        got[v, :, c] = mid[v, :, c]

    send_y(0)
    to_below = remote(ctl_ref, up_raw, halo_send.at[0], halo_recv.at[0], (g, below))
    to_above = remote(ctl_ref, dn_raw, halo_send.at[1], halo_recv.at[1], (g, above))
    to_below.start()
    to_above.start()
    send_y(1)
    for v in range(VAR):
        mid[v, y] = packed[v, y]

    loads[4].wait()
    loads[5].wait()

    level = lax.broadcasted_iota(jnp.int32, (LEV, LANES), 0)
    rate = jnp.zeros((LEV, LANES), jnp.float32)
    count = jnp.zeros((LEV, LANES), jnp.int32)
    for l in range(LEV):
        rate = jnp.where(level == l, rate_ref[l], rate)
        count = jnp.where(level == l, steps_ref[l], count)
    has_up = jnp.where(d > 0, 1.0, 0.0).astype(jnp.float32)
    has_dn = jnp.where(d < NDOM - 1, 1.0, 0.0).astype(jnp.float32)
    for s in range(NSTEP):
        now = jnp.where(s < count, rate, 0.0)
        coef[3 * s] = now
        coef[3 * s + 1] = now * has_up
        coef[3 * s + 2] = now * has_dn

    def fill(source, base_row):
        def body(n, carry):
            m, i = n // ROWS, lax.rem(n, ROWS)
            for t in range(TILES):
                ext[m, base_row + i, :, t * LANES : (t + 1) * LANES] = source[
                    pl.ds(m * 256 + t * ROWS + i, LEV, stride=32), :
                ]
            return carry

        lax.fori_loop(0, MEM * ROWS, body, 0)

    def clear(buffer, base_row):
        for m in range(MEM):
            for i in range(ROWS):
                buffer[m, base_row + i] = jnp.zeros((LEV, LON), jnp.float32)

    fill(ctl_ref, ROWS)
    send_z(0)
    send_z(1)

    to_below.wait_recv()
    fill(up_raw, 0)
    to_above.wait_recv()
    fill(dn_raw, 2 * ROWS)

    @pl.when(d == 0)
    def _():
        clear(ext, 0)

    @pl.when(d == NDOM - 1)
    def _():
        clear(ext, 2 * ROWS)

    def localize(m, carry):
        def emit(i, value):
            loc[m * ROWS + i] = value

        sweeps(ext, tmp, coef, m, emit)
        return carry

    lax.fori_loop(0, MEM, localize, 0)

    slot = lane_iota((LEV, LANES)) // SLOT
    masks = {step: (slot & step) != 0 for step in (4, 2, 1)}

    for v in range(VAR):
        wait_bytes(got.at[v, pl.ds(0, TILES - 1)], z_recv.at[v])

        def relayout(t, carry):
            tiles = [got[v, t, n].astype(jnp.float32) for n in range(TILES)]
            for step in (4, 2, 1):
                high = masks[step]
                for a in range(TILES):
                    if a & step:
                        continue
                    p, q = tiles[a], tiles[a + step]
                    tiles[a] = jnp.where(high, pltpu.roll(q, step * SLOT, axis=1), p)
                    tiles[a + step] = jnp.where(
                        high, q, pltpu.roll(p, LANES - step * SLOT, axis=1)
                    )
            for k in range(TILES):
                pert[v, t, k] = tiles[k]
            cols = pl.ds(pl.multiple_of(t * LANES, LANES), LANES)
            for i in range(ROWS):
                part[2 * v + t // 4, 4 * i + lax.rem(t, 4)] = (
                    tiles[i] * loc[i, :, cols] + tiles[ROWS + i] * loc[ROWS + i, :, cols]
                )
            return carry

        lax.fori_loop(0, TILES, relayout, 0, unroll=2)
        for q in (2 * v, 2 * v + 1):
            for k in FAR_FIRST_16:
                to = lax.rem(g + k, NGRP)
                remote(
                    part.at[q, to], red.at[q, g], rs_send.at[q], rs_recv.at[q], (to, d)
                ).start()
            red[q, g] = part[q, g]

    for q in range(2 * VAR):
        wait_bytes(red.at[q, pl.ds(0, NGRP - 1)], rs_recv.at[q])
        total = red[q, 0]
        for n in range(1, NGRP):
            total = total + red[q, n]
        incs[q, g] = total * factor
        for k in FAR_FIRST_16:
            remote(
                incs.at[q, g],
                incs.at[q, g],
                ag_send.at[q],
                ag_recv.at[q],
                (lax.rem(g + k, NGRP), d),
            ).start()

    loads[2].wait()
    loads[3].wait()
    copies = []
    for h in range(2):
        for v in range(VAR):
            wait_bytes(incs.at[2 * v + h, pl.ds(0, NGRP - 1)], ag_recv.at[2 * v + h])

        def back(i, carry):
            for n in range(TILES // 2):
                t = h * (TILES // 2) + n
                cols = slice(t * LANES, (t + 1) * LANES)
                res = []
                for v in range(VAR):
                    lines = pl.ds(v * 32 + t * ROWS + i, LEV, stride=64)
                    inc = incs[2 * v + h, 4 * i + n]
                    inc_ref[lines, :] = inc
                    res.append(wgt_ref[lines, :] * (inc - dep_ref[lines, :]))
                for m in range(MEM):
                    ext2[m, ROWS + i, :, cols] = (
                        pert[0, t, m * ROWS + i] * res[0] + pert[1, t, m * ROWS + i] * res[1]
                    ) * factor
            return carry

        lax.fori_loop(0, ROWS, back, 0)
        cols = pl.ds(h * HALF, HALF)
        own = ext2.at[:, pl.ds(ROWS, ROWS), :, cols]
        for n, (row, to) in enumerate(((0, below), (2 * ROWS, above))):
            copies.append(
                remote(
                    own,
                    ext2.at[:, pl.ds(row, ROWS), :, cols],
                    adj_send.at[2 * h + n],
                    adj_recv.at[2 * h + n],
                    (g, to),
                )
            )
            copies[-1].start()

    to_below.wait_send()
    to_above.wait_send()
    for v in range(VAR):
        wait_bytes(packed.at[v, pl.ds(0, TILES - 1)], y_send.at[v])
        wait_bytes(mid.at[v, pl.ds(0, TILES - 1)], z_send.at[v])
    for q in range(2 * VAR):
        wait_bytes(part.at[q, pl.ds(0, NGRP - 1)], rs_send.at[q])
        wait_bytes(incs.at[q, pl.ds(0, NGRP - 1)], ag_send.at[q])
    for copy in copies:
        copy.wait()

    @pl.when(d == 0)
    def _():
        clear(ext2, 0)

    @pl.when(d == NDOM - 1)
    def _():
        clear(ext2, 2 * ROWS)

    def gradient(m, carry):
        def emit(i, value):
            for t in range(TILES):
                lines = pl.ds(m * 256 + t * ROWS + i, LEV, stride=32)
                grad_ref[lines, :] = ctl_ref[lines, :] + value[:, t * LANES : (t + 1) * LANES]

        sweeps(ext2, tmp, coef, m, emit)
        return carry

    lax.fori_loop(0, MEM, gradient, 0)


def tiles_of(x):
    a, b, rows, lon = x.shape
    return (
        x.reshape(a, b, rows, lon // LANES, LANES)
        .transpose(0, 1, 3, 2, 4)
        .reshape(a * b * rows * lon // LANES, LANES)
    )


def from_tiles(x, shape):
    a, b, rows, lon = shape
    return (
        x.reshape(a, b, lon // LANES, rows, LANES).transpose(0, 1, 3, 2, 4).reshape(shape)
    )


def pin(x):
    return pltpu.with_memory_space_constraint(x, pltpu.HBM)


def per_device(pert_fcst, control, departures, obs_weight, diff_rate, step_counts):
    members = MEM * lax.axis_size("grp")
    factor = 1.0 / math.sqrt(members - 1)
    pert = (
        pert_fcst.reshape(MEM, LEV, VAR, 32, LANES)
        .transpose(0, 1, 3, 2, 4)
        .reshape(MEM * LEV * 32 * VAR, LANES)
    )
    vmem = pl.BlockSpec(memory_space=pltpu.VMEM)
    flat = (MEM * LEV * ROWS * TILES, LANES)
    f32, bf16 = jnp.float32, jnp.bfloat16
    hbm = pl.BlockSpec(memory_space=pltpu.HBM)
    dma = pltpu.SemaphoreType.DMA
    inc, grad = pl.pallas_call(
        functools.partial(kernel, factor),
        out_shape=(jax.ShapeDtypeStruct(flat, f32), jax.ShapeDtypeStruct(flat, f32)),
        in_specs=[hbm] * 6,
        out_specs=(vmem, vmem),
        scratch_shapes=[
            pltpu.SMEM((LEV,), f32),
            pltpu.SMEM((LEV,), jnp.int32),
            pltpu.VMEM((1024, LANES), bf16),
            pltpu.VMEM(flat, f32),
            pltpu.VMEM(flat, f32),
            pltpu.VMEM(flat, f32),
            pltpu.VMEM((1024, LANES), f32),
            pltpu.VMEM((VAR, TILES, TILES, LEV, LANES), bf16),
            pltpu.VMEM((VAR, TILES, TILES, LEV, LANES), bf16),
            pltpu.VMEM((VAR, TILES, TILES, LEV, LANES), bf16),
            pltpu.VMEM((VAR, TILES, MEM * ROWS, LEV, LANES), f32),
            pltpu.VMEM(flat, f32),
            pltpu.VMEM(flat, f32),
            pltpu.VMEM((MEM, 3 * ROWS, LEV, LON), f32),
            pltpu.VMEM((MEM, 3 * ROWS, LEV, LON), f32),
            pltpu.VMEM((MEM, 3 * ROWS, LEV, LON), f32),
            pltpu.VMEM((MEM * ROWS, LEV, LON), f32),
            pltpu.VMEM((3 * NSTEP, LEV, LANES), f32),
            pltpu.VMEM((2 * VAR, NGRP, LEV, LANES), f32),
            pltpu.VMEM((2 * VAR, NGRP, LEV, LANES), f32),
            pltpu.VMEM((2 * VAR, NGRP, LEV, LANES), f32),
            dma((6,)),
            dma((2,)),
            dma((2,)),
            dma((2,)),
            dma((2,)),
            dma((2,)),
            dma((2,)),
            dma((4,)),
            dma((4,)),
            dma((4,)),
            dma((4,)),
            dma((4,)),
            dma((4,)),
        ],
        compiler_params=pltpu.CompilerParams(
            collective_id=0, has_side_effects=True, vmem_limit_bytes=48 * 1024 * 1024
        ),
    )(
        pin(diff_rate),
        pin(step_counts),
        pin(pert),
        pin(tiles_of(control)),
        pin(tiles_of(departures)),
        pin(tiles_of(obs_weight)),
    )
    return (from_tiles(inc, (LEV, VAR, ROWS, LON)), from_tiles(grad, (MEM, LEV, ROWS, LON)))


def solution(mesh):
    in_specs = (
        P("grp", None, None, "dom", None),
        P("grp", None, "dom", None),
        P(None, None, "dom", None),
        P(None, None, "dom", None),
        P(),
        P(),
    )
    out_specs = (P(None, None, "dom", None), P("grp", None, "dom", None))
    return jax.shard_map(
        per_device, mesh=mesh, in_specs=in_specs, out_specs=out_specs, check_vma=False
    )
```

time: 77.6 us -> 66.3 us (0.85)
  Pallas kernels: 70.8 us -> 64.1 us
  local copies, waits for them, and re-layouts: 5.86 us -> 1.41 us
    pallas_call x1, Pallas kernels: 70.8 us -> 64.1 us  [per_device(): pl.pallas_call(functools.partial(kernel, factor), out_shape=(jax.ShapeDty...]
    unnamed x14 -> x2, local copies, waits for them, and re-layouts: 5.86 us -> 1.41 us
where the time goes in v2:
time: 66.3 us; the launch traced here: 66.2 us
  Pallas kernels  64.1 us (97%)
  local copies, waits for them, and re-layouts  1.41 us (2%)
    pallas_call x1, Pallas kernels, per_device(): pl.pallas_call(functools.partial(kernel, factor), out_shape=(jax.ShapeDty...  64.1 us
    unnamed x2, local copies, waits for them, and re-layouts  1.41 us

profile of v2, /device:TPU:1, one launch (start us, length us, event | category | flops | bytes accessed | tf_op | source)
XLA Modules:
  0.0 66.2 jit_solution(6327468620618471774)
XLA Ops:
  0.6 64.1 %shard_map.77 = (f32[512,128]{1,0:T(8,128)S(1)}, f32[512,128]{1,0:T(8,128)S(1)}) custom-call(f32[8]{0:T(128)} %rate_hbm.1, s32[8]{0:T(128)} %steps_hbm.1, bf16[1024,128]{1,0:T(8,128)(2,1)} %bitcast.32, f32[512,128]{1,0:T(8,128)} %bitcast.33, f32[512,128]{1,0:T(8,128)} %bitcast.34, f32[512,128]{1,0:T(8,128)} %bitcast.35), custom_call_target="tpu_custom_call" | custom-call | tf_op jit(solution)/shard_map/pallas_call | solution.py:431
  64.8 0.7 %copy.16 = f32[8,2,4,1024]{3,2,1,0:T(4,128)} copy(f32[8,2,4,1024]{3,2,1,0:T(4,128)S(1)} %bitcast.31) | data formatting | bytes 524288
  65.5 0.7 %copy.17 = f32[2,8,4,1024]{3,2,1,0:T(4,128)} copy(f32[2,8,4,1024]{3,2,1,0:T(4,128)S(1)} %bitcast.30) | data formatting | bytes 524288

commit v3 on v2

--- a/solution.py
+++ b/solution.py
@@ -106,10 +106,10 @@
     red,
     incs,
     load_sem,
-    y_send,
-    y_recv,
-    z_send,
-    z_recv,
+    one_send,
+    one_recv,
+    two_send,
+    two_recv,
     halo_send,
     halo_recv,
     rs_send,
@@ -187,35 +187,42 @@
     ends = c // (TILES - 1) + (TILES - 1 - c) // (TILES - 1)
     pl.semaphore_wait(barrier, 2 * (TILES - 1) + NGRP - 1 + ends)
 
-    def send_y(v):
+    def first_stage(v, k):
+        if v == 0:
+            to = y_mate(k)
+            src, dst, device = packed.at[v, to], mid.at[v, y], (g, to * TILES + c)
+        else:
+            to = z_mate(k)
+            src, dst, device = packed.at[v, :, to], mid.at[v, :, c], (g, y * TILES + to)
+        remote(src, dst, one_send.at[v], one_recv.at[v], device).start()
+
+    def second_stage(v, k):
+        if v == 0:
+            to = z_mate(k)
+            src, dst, device = mid.at[v, :, to], got.at[v, :, c], (g, y * TILES + to)
+        else:
+            to = y_mate(k)
+            src, dst, device = mid.at[v, to], got.at[v, y], (g, to * TILES + c)
+        remote(src, dst, two_send.at[v], two_recv.at[v], device).start()
+
+    def forward(v):
+        wait_bytes(mid.at[v, pl.ds(0, TILES - 1)], one_recv.at[v])
         for k in FAR_FIRST_8:
-            to = y_mate(k)
-            remote(
-                packed.at[v, to], mid.at[v, y], y_send.at[v], y_recv.at[v], (g, to * TILES + c)
-            ).start()
-
-    def send_z(v):
-        wait_bytes(mid.at[v, pl.ds(0, TILES - 1)], y_recv.at[v])
-        for k in FAR_FIRST_8:
-            to = z_mate(k)
-            remote(
-                mid.at[v, :, to],
-                got.at[v, :, c],
-                z_send.at[v],
-                z_recv.at[v],
-                (g, y * TILES + to),
-            ).start()
-        got[v, :, c] = mid[v, :, c]
-
-    send_y(0)
+            second_stage(v, k)
+        if v == 0:
+            got[v, :, c] = mid[v, :, c]
+        else:
+            got[v, y] = mid[v, y]
+
+    for k in FAR_FIRST_8:
+        for v in range(VAR):
+            first_stage(v, k)
     to_below = remote(ctl_ref, up_raw, halo_send.at[0], halo_recv.at[0], (g, below))
     to_above = remote(ctl_ref, dn_raw, halo_send.at[1], halo_recv.at[1], (g, above))
     to_below.start()
     to_above.start()
-    send_y(1)
-    for v in range(VAR):
-        mid[v, y] = packed[v, y]
-
+    mid[0, y] = packed[0, y]
+    mid[1, :, c] = packed[1, :, c]
     loads[4].wait()
     loads[5].wait()
 
@@ -250,8 +257,8 @@
                 buffer[m, base_row + i] = jnp.zeros((LEV, LON), jnp.float32)
 
     fill(ctl_ref, ROWS)
-    send_z(0)
-    send_z(1)
+    forward(0)
+    forward(1)
 
     to_below.wait_recv()
     fill(up_raw, 0)
@@ -279,7 +286,7 @@
     masks = {step: (slot & step) != 0 for step in (4, 2, 1)}
 
     for v in range(VAR):
-        wait_bytes(got.at[v, pl.ds(0, TILES - 1)], z_recv.at[v])
+        wait_bytes(got.at[v, pl.ds(0, TILES - 1)], two_recv.at[v])
 
         def relayout(t, carry):
             tiles = [got[v, t, n].astype(jnp.float32) for n in range(TILES)]
@@ -367,8 +374,8 @@
     to_below.wait_send()
     to_above.wait_send()
     for v in range(VAR):
-        wait_bytes(packed.at[v, pl.ds(0, TILES - 1)], y_send.at[v])
-        wait_bytes(mid.at[v, pl.ds(0, TILES - 1)], z_send.at[v])
+        wait_bytes(packed.at[v, pl.ds(0, TILES - 1)], one_send.at[v])
+        wait_bytes(mid.at[v, pl.ds(0, TILES - 1)], two_send.at[v])
     for q in range(2 * VAR):
         wait_bytes(part.at[q, pl.ds(0, NGRP - 1)], rs_send.at[q])
         wait_bytes(incs.at[q, pl.ds(0, NGRP - 1)], ag_send.at[q])

time: 66.3 us -> 64.9 us (0.979)
  Pallas kernels: 64.1 us -> 62.7 us
    pallas_call x1, Pallas kernels: 64.1 us -> 62.7 us  [per_device(): pl.pallas_call(functools.partial(kernel, factor), out_shape=(jax.ShapeDty...]
where the time goes in v3:
time: 64.9 us; the launch traced here: 64.8 us
  Pallas kernels  62.7 us (97%)
  local copies, waits for them, and re-layouts  1.41 us (2%)
    pallas_call x1, Pallas kernels, per_device(): pl.pallas_call(functools.partial(kernel, factor), out_shape=(jax.ShapeDty...  62.7 us
    unnamed x2, local copies, waits for them, and re-layouts  1.41 us

profile of v3, /device:TPU:1, one launch (start us, length us, event | category | flops | bytes accessed | tf_op | source)
XLA Modules:
  0.0 64.8 jit_solution(6915662308988433299)
XLA Ops:
  0.6 62.7 %shard_map.77 = (f32[512,128]{1,0:T(8,128)S(1)}, f32[512,128]{1,0:T(8,128)S(1)}) custom-call(f32[8]{0:T(128)} %rate_hbm.1, s32[8]{0:T(128)} %steps_hbm.1, bf16[1024,128]{1,0:T(8,128)(2,1)} %bitcast.32, f32[512,128]{1,0:T(8,128)} %bitcast.33, f32[512,128]{1,0:T(8,128)} %bitcast.34, f32[512,128]{1,0:T(8,128)} %bitcast.35), custom_call_target="tpu_custom_call" | custom-call | tf_op jit(solution)/shard_map/pallas_call | solution.py:438
  63.3 0.7 %copy.16 = f32[8,2,4,1024]{3,2,1,0:T(4,128)} copy(f32[8,2,4,1024]{3,2,1,0:T(4,128)S(1)} %bitcast.31) | data formatting | bytes 524288
  64.1 0.7 %copy.17 = f32[2,8,4,1024]{3,2,1,0:T(4,128)} copy(f32[2,8,4,1024]{3,2,1,0:T(4,128)S(1)} %bitcast.30) | data formatting | bytes 524288

commit v4 on v3

--- a/solution.py
+++ b/solution.py
@@ -95,11 +95,15 @@
     mid,
     got,
     pert,
-    up_raw,
-    dn_raw,
     ext,
+    own16,
+    up16,
+    dn16,
     tmp,
     ext2,
+    own16b,
+    up16b,
+    dn16b,
     loc,
     coef,
     part,
@@ -217,12 +221,18 @@
     for k in FAR_FIRST_8:
         for v in range(VAR):
             first_stage(v, k)
-    to_below = remote(ctl_ref, up_raw, halo_send.at[0], halo_recv.at[0], (g, below))
-    to_above = remote(ctl_ref, dn_raw, halo_send.at[1], halo_recv.at[1], (g, above))
-    to_below.start()
-    to_above.start()
     mid[0, y] = packed[0, y]
     mid[1, :, c] = packed[1, :, c]
+    def fill(n, carry):
+        m, i = n // ROWS, lax.rem(n, ROWS)
+        for t in range(TILES):
+            cols = slice(t * LANES, (t + 1) * LANES)
+            tile = ctl_ref[pl.ds(m * 256 + t * ROWS + i, LEV, stride=32), :]
+            ext[m, ROWS + i, :, cols] = tile
+            own16[m, i, :, cols] = tile.astype(jnp.bfloat16)
+        return carry
+
+    lax.fori_loop(0, MEM * ROWS, fill, 0)
     loads[4].wait()
     loads[5].wait()
 
@@ -240,30 +250,40 @@
         coef[3 * s + 1] = now * has_up
         coef[3 * s + 2] = now * has_dn
 
-    def fill(source, base_row):
-        def body(n, carry):
-            m, i = n // ROWS, lax.rem(n, ROWS)
-            for t in range(TILES):
-                ext[m, base_row + i, :, t * LANES : (t + 1) * LANES] = source[
-                    pl.ds(m * 256 + t * ROWS + i, LEV, stride=32), :
-                ]
-            return carry
-
-        lax.fori_loop(0, MEM * ROWS, body, 0)
-
     def clear(buffer, base_row):
         for m in range(MEM):
             for i in range(ROWS):
                 buffer[m, base_row + i] = jnp.zeros((LEV, LON), jnp.float32)
 
-    fill(ctl_ref, ROWS)
+    def halo(field, mine, up, dn, cols, send, recv):
+        pairs = (
+            (field.at[:, pl.ds(6, 2), :, cols], field.at[:, pl.ds(2, 2), :, cols], below),
+            (field.at[:, pl.ds(4, 2), :, cols], field.at[:, pl.ds(8, 2), :, cols], above),
+            (mine.at[:, pl.ds(0, 2), :, cols], up.at[:, :, :, cols], below),
+            (mine.at[:, pl.ds(2, 2), :, cols], dn.at[:, :, :, cols], above),
+        )
+        copies = [
+            remote(src, dst, send.at[n], recv.at[n], (g, to))
+            for n, (src, dst, to) in enumerate(pairs)
+        ]
+        for copy in copies:
+            copy.start()
+        return copies
+
+    def widen(field, up, dn):
+        for m in range(MEM):
+            for i in range(2):
+                field[m, i] = up[m, i].astype(jnp.float32)
+                field[m, 10 + i] = dn[m, i].astype(jnp.float32)
+
+    everything = pl.ds(0, LON)
+    copies = halo(ext, own16, up16, dn16, everything, halo_send, halo_recv)
     forward(0)
     forward(1)
 
-    to_below.wait_recv()
-    fill(up_raw, 0)
-    to_above.wait_recv()
-    fill(dn_raw, 2 * ROWS)
+    for copy in copies:
+        copy.wait()
+    widen(ext, up16, dn16)
 
     @pl.when(d == 0)
     def _():
@@ -351,28 +371,19 @@
                     inc_ref[lines, :] = inc
                     res.append(wgt_ref[lines, :] * (inc - dep_ref[lines, :]))
                 for m in range(MEM):
-                    ext2[m, ROWS + i, :, cols] = (
+                    adj = (
                         pert[0, t, m * ROWS + i] * res[0] + pert[1, t, m * ROWS + i] * res[1]
                     ) * factor
+                    ext2[m, ROWS + i, :, cols] = adj
+                    own16b[m, i, :, cols] = adj.astype(jnp.bfloat16)
             return carry
 
         lax.fori_loop(0, ROWS, back, 0)
         cols = pl.ds(h * HALF, HALF)
-        own = ext2.at[:, pl.ds(ROWS, ROWS), :, cols]
-        for n, (row, to) in enumerate(((0, below), (2 * ROWS, above))):
-            copies.append(
-                remote(
-                    own,
-                    ext2.at[:, pl.ds(row, ROWS), :, cols],
-                    adj_send.at[2 * h + n],
-                    adj_recv.at[2 * h + n],
-                    (g, to),
-                )
-            )
-            copies[-1].start()
-
-    to_below.wait_send()
-    to_above.wait_send()
+        copies += halo(
+            ext2, own16b, up16b, dn16b, cols, adj_send.at[pl.ds(4 * h, 4)], adj_recv.at[pl.ds(4 * h, 4)]
+        )
+
     for v in range(VAR):
         wait_bytes(packed.at[v, pl.ds(0, TILES - 1)], one_send.at[v])
         wait_bytes(mid.at[v, pl.ds(0, TILES - 1)], two_send.at[v])
@@ -381,6 +392,7 @@
         wait_bytes(incs.at[q, pl.ds(0, NGRP - 1)], ag_send.at[q])
     for copy in copies:
         copy.wait()
+    widen(ext2, up16b, dn16b)
 
     @pl.when(d == 0)
     def _():
@@ -452,11 +464,15 @@
             pltpu.VMEM((VAR, TILES, TILES, LEV, LANES), bf16),
             pltpu.VMEM((VAR, TILES, TILES, LEV, LANES), bf16),
             pltpu.VMEM((VAR, TILES, MEM * ROWS, LEV, LANES), f32),
-            pltpu.VMEM(flat, f32),
-            pltpu.VMEM(flat, f32),
+            pltpu.VMEM((MEM, 3 * ROWS, LEV, LON), f32),
+            pltpu.VMEM((MEM, ROWS, LEV, LON), bf16),
+            pltpu.VMEM((MEM, 2, LEV, LON), bf16),
+            pltpu.VMEM((MEM, 2, LEV, LON), bf16),
             pltpu.VMEM((MEM, 3 * ROWS, LEV, LON), f32),
             pltpu.VMEM((MEM, 3 * ROWS, LEV, LON), f32),
-            pltpu.VMEM((MEM, 3 * ROWS, LEV, LON), f32),
+            pltpu.VMEM((MEM, ROWS, LEV, LON), bf16),
+            pltpu.VMEM((MEM, 2, LEV, LON), bf16),
+            pltpu.VMEM((MEM, 2, LEV, LON), bf16),
             pltpu.VMEM((MEM * ROWS, LEV, LON), f32),
             pltpu.VMEM((3 * NSTEP, LEV, LANES), f32),
             pltpu.VMEM((2 * VAR, NGRP, LEV, LANES), f32),
@@ -467,14 +483,14 @@
             dma((2,)),
             dma((2,)),
             dma((2,)),
-            dma((2,)),
-            dma((2,)),
             dma((4,)),
             dma((4,)),
             dma((4,)),
             dma((4,)),
             dma((4,)),
             dma((4,)),
+            dma((8,)),
+            dma((8,)),
         ],
         compiler_params=pltpu.CompilerParams(
             collective_id=0, has_side_effects=True, vmem_limit_bytes=48 * 1024 * 1024

time: 64.9 us -> 62.1 us (0.957)
  Pallas kernels: 62.7 us -> 59.9 us
    pallas_call x1, Pallas kernels: 62.7 us -> 59.9 us  [per_device(): pl.pallas_call(functools.partial(kernel, factor), out_shape=(jax.ShapeDty...]
where the time goes in v4:
time: 62.1 us; the launch traced here: 62 us
  Pallas kernels  59.9 us (96%)
  local copies, waits for them, and re-layouts  1.41 us (2%)
  between operations  0.64 us (1%)
    pallas_call x1, Pallas kernels, per_device(): pl.pallas_call(functools.partial(kernel, factor), out_shape=(jax.ShapeDty...  59.9 us
    unnamed x2, local copies, waits for them, and re-layouts  1.41 us

profile of v4, /device:TPU:1, one launch (start us, length us, event | category | flops | bytes accessed | tf_op | source)
XLA Modules:
  0.0 62.0 jit_solution(1682606120619367276)
XLA Ops:
  0.6 59.9 %shard_map.77 = (f32[512,128]{1,0:T(8,128)S(1)}, f32[512,128]{1,0:T(8,128)S(1)}) custom-call(f32[8]{0:T(128)} %rate_hbm.1, s32[8]{0:T(128)} %steps_hbm.1, bf16[1024,128]{1,0:T(8,128)(2,1)} %bitcast.32, f32[512,128]{1,0:T(8,128)} %bitcast.33, f32[512,128]{1,0:T(8,128)} %bitcast.34, f32[512,128]{1,0:T(8,128)} %bitcast.35), custom_call_target="tpu_custom_call" | custom-call | tf_op jit(solution)/shard_map/pallas_call | solution.py:450
  60.6 0.7 %copy.16 = f32[8,2,4,1024]{3,2,1,0:T(4,128)} copy(f32[8,2,4,1024]{3,2,1,0:T(4,128)S(1)} %bitcast.31) | data formatting | bytes 524288
  61.3 0.7 %copy.17 = f32[2,8,4,1024]{3,2,1,0:T(4,128)} copy(f32[2,8,4,1024]{3,2,1,0:T(4,128)S(1)} %bitcast.30) | data formatting | bytes 524288
